TPU v7x, 32 devices: a whole 2x2x4 slice. The times are simulated.
32 devices in a mesh: groups: 2 (over y), samples: 8 (over z, x), section: 1, mp: 2 (over core).
Axes of the slice: x: 2, y: 2, z: 4, core: 2. Of those that a mesh axis runs over, the one named last changes fastest.
Arguments:
- stored_inputs: bfloat16 [1, 16, 128, 2048], P('section', ('groups', 'samples'), None, 'mp'), parts along dimension 1
- top_cotangent: bfloat16 [16, 128, 2048], P(('groups', 'samples'), None, 'mp'), parts along dimension 0, may hold values from -0.375 to 0.375
- layer_weights: bfloat16 [1, 2048, 2048], P('section', 'samples', 'mp'), may hold values from -0.125 to 0.125
- block_layout: int32 [1, 2, 2], P('section'), may hold values 0 or 1
- region_mask: int32 [128], replicated, may hold values from 0 to 1, as said below
- partner_samples: int32 [16], P('groups'), parts along dimension 0, may hold values from 0 to 7, as said below
- spins: int32 [16, 128], P(('groups', 'samples')), parts along dimension 0, may hold values from 0 to 1
Outputs:
- weight_grad: float32 [2, 2048, 2048], P(('groups', 'section'), 'samples', 'mp'), parts along dimension 0
- layer_cotangents: bfloat16 [1, 16, 128, 2048], P('section', ('groups', 'samples'), None, 'mp'), parts along dimension 1
- embed_grad: float32 [4, 2048], P('groups', 'mp'), parts along dimension 0
There are 2 independent parts, one for each index of `groups`. A program takes and returns all parts, laid end to end along the dimension named above; an argument that names none is the same for every part. Nothing has to cross between parts.
Inputs may be any that keep to these rules, and one draw needn't show every extreme that they name: `region_mask`: exactly 64 of the 128 entries are 1, the others 0. The samples pair up: partner_samples[partner_samples[r]] = r and partner_samples[r] != r for every sample r. `block_layout`: a query block always sees its own block, whatever the diagonal entry holds.
All inputs are finite; a program needn't handle non-finite values.
Results may differ from a plain program's by a relative error of at most 0.03.
Values may be sent and summed in bfloat16 or wider, within the bound.
A program may use at most 64 MiB of HBM per device.

v0:
```python
import jax
import jax.numpy as jnp
from jax import lax
from jax.sharding import PartitionSpec as P

HEAD = 128
BLOCK = 64
SPINS = 2


def for_sending(value):

    def short(part):
        return part.astype(jnp.bfloat16) if part.dtype == jnp.float32 else part

    return jax.tree.map(short, value)


def passed_along(block, axis, distance):
    devices = range(lax.axis_size(axis))
    route = [(i - distance, i) for i in devices if i - distance in devices]
    return lax.ppermute(block, axis, route)


def softmax_parts(inputs_h, allowed, attention_scale):
    scores = (
        jnp.einsum("qhd,khd->hqk", inputs_h, inputs_h, preferred_element_type=jnp.float32)
        * attention_scale
    )
    scores = jnp.where(allowed[None], scores, -jnp.inf)
    top_score = jnp.max(scores, axis=-1, keepdims=True)
    expo_terms = jnp.exp(scores - top_score)
    probs = expo_terms / jnp.sum(expo_terms, axis=-1, keepdims=True)
    return (probs, probs.astype(jnp.bfloat16))


def local(
    stored_inputs, top_cotangent, layer_weights, block_layout, region_mask, partner_samples, spins
):
    section_index = lax.axis_index("section")
    section_count = lax.axis_size("section")
    micro_count = stored_inputs.shape[1]
    seq_len = stored_inputs.shape[2]
    half_width = stored_inputs.shape[3]
    head_count = half_width // HEAD
    attention_scale = 4.0 / HEAD
    weights = lax.all_gather(layer_weights[0], "samples", axis=0, tiled=True)
    pos_block = jnp.arange(seq_len) // BLOCK
    block_onehot = (pos_block[:, None] == jnp.arange(block_layout.shape[1])[None, :]).astype(
        jnp.float32
    )
    linked = jnp.dot(jnp.dot(block_onehot, block_layout[0].astype(jnp.float32)), block_onehot.T)
    allowed = (linked > 0.5) | (pos_block[:, None] == pos_block[None, :])
    every_layer_input = stored_inputs[0]
    inputs_h = every_layer_input[0].reshape(seq_len, head_count, HEAD)
    probs, probs_low = softmax_parts(inputs_h, allowed, attention_scale)
    attended = jnp.einsum(
        "hqk,khd->qhd", probs_low, inputs_h, preferred_element_type=jnp.float32
    ).astype(jnp.bfloat16)
    probs_list = [probs]
    low_list = [probs_low]
    attend_list = [attended.reshape(seq_len, half_width)]
    probs_all = jnp.stack(probs_list)
    low_all = jnp.stack(low_list)
    attend_store = jnp.stack(attend_list)

    def layer_back(grad_full, grad_own, inputs, probs, probs_low):
        grad_attn = jnp.dot(grad_full, weights, preferred_element_type=jnp.float32).astype(
            jnp.bfloat16
        )
        inputs_h = inputs.reshape(seq_len, head_count, HEAD)
        grad_h = grad_attn.reshape(seq_len, head_count, HEAD)
        grad_probs = jnp.einsum(
            "qhd,khd->hqk", grad_h, inputs_h, preferred_element_type=jnp.float32
        )
        grad_scores = (
            probs * (grad_probs - jnp.sum(grad_probs * probs, axis=-1, keepdims=True))
        ).astype(jnp.bfloat16)
        through = jnp.einsum("hqk,qhd->khd", probs_low, grad_h, preferred_element_type=jnp.float32)
        through = through + attention_scale * (
            jnp.einsum("hqk,khd->qhd", grad_scores, inputs_h, preferred_element_type=jnp.float32)
            + jnp.einsum("hqk,qhd->khd", grad_scores, inputs_h, preferred_element_type=jnp.float32)
        )
        grad_in = grad_own.astype(jnp.float32) + through.reshape(seq_len, half_width)
        return grad_in.astype(jnp.bfloat16)

    def resting(grad_full, grad_own, inputs, probs, probs_low):
        return jnp.zeros((seq_len, half_width), jnp.bfloat16)

    carried_state = jnp.zeros((seq_len, half_width), jnp.bfloat16)
    out_list = []
    grad_list = []
    total_steps = micro_count + section_count - 1
    for step_number in range(total_steps):
        micro_index = step_number - (section_count - 1 - section_index)
        active = (micro_index >= 0) & (micro_index < micro_count)
        slot_index = jnp.clip(micro_index, 0, micro_count - 1)
        from_top = lax.dynamic_index_in_dim(top_cotangent, slot_index, 0, keepdims=False)
        incoming = jnp.where(section_index == section_count - 1, from_top, carried_state)
        grad_full = lax.all_gather(incoming, "mp", axis=1, tiled=True)
        inputs_now = lax.dynamic_index_in_dim(every_layer_input, slot_index, 0, keepdims=False)
        probs_now = lax.dynamic_index_in_dim(probs_all, slot_index, 0, keepdims=False)
        low_now = lax.dynamic_index_in_dim(low_all, slot_index, 0, keepdims=False)
        grad_in = lax.cond(
            active, layer_back, resting, grad_full, incoming, inputs_now, probs_now, low_now
        )
        out_list.append(grad_in)
        grad_list.append(grad_full)
        if step_number < total_steps - 1:
            carried_state = jax.tree.map(
                lambda part, own: part.astype(own.dtype),
                passed_along(for_sending(grad_in), "section", -1),
                grad_in,
            )
    offset = section_count - 1 - section_index
    out_store = lax.dynamic_slice_in_dim(jnp.stack(out_list), offset, micro_count, 0)
    grad_store = lax.dynamic_slice_in_dim(jnp.stack(grad_list), offset, micro_count, 0)
    summed_weight = lax.psum_scatter(
        jnp.einsum(
            "mtf,mta->fa", grad_store, attend_store, preferred_element_type=jnp.float32
        ).astype(jnp.bfloat16),
        "samples",
        scatter_dimension=0,
        tiled=True,
    ).astype(jnp.float32)
    region_count = seq_len // 2
    rank_in_region = jnp.cumsum(region_mask) - 1
    select = (
        (rank_in_region[None, :] == jnp.arange(region_count)[:, None]) & (region_mask[None, :] > 0)
    ).astype(jnp.bfloat16)
    tiles = jnp.einsum("at,mtd->mad", select, out_store, preferred_element_type=jnp.float32).astype(
        jnp.bfloat16
    )
    shard_index = lax.axis_index("samples")
    my_partners = lax.dynamic_slice_in_dim(
        partner_samples, shard_index * micro_count, micro_count, 0
    )
    shard_count = lax.axis_size("samples")
    dest_shard = my_partners // micro_count
    dest_slot = my_partners % micro_count
    route = (
        (dest_shard[:, None, None] == jnp.arange(shard_count)[None, :, None])
        & (dest_slot[:, None, None] == jnp.arange(micro_count)[None, None, :])
    ).astype(jnp.bfloat16)
    outgoing = jnp.einsum("mku,mad->kuad", route, tiles, preferred_element_type=jnp.float32).astype(
        jnp.bfloat16
    )
    arrived = lax.all_to_all(outgoing, "samples", split_axis=0, concat_axis=0, tiled=True)
    ones_row = jnp.ones((shard_count,), jnp.bfloat16)
    received = jnp.einsum(
        "k,kuad->uad", ones_row, arrived, preferred_element_type=jnp.float32
    ).astype(jnp.bfloat16)
    placed = jnp.einsum("at,mad->mtd", select, received, preferred_element_type=jnp.float32)
    kept = jnp.where(region_mask[None, :, None] > 0, jnp.zeros_like(out_store), out_store)
    site_cot = (kept.astype(jnp.float32) + placed).astype(jnp.bfloat16)
    cotangents = jnp.where(section_index == 0, site_cot, out_store)
    onehot = (spins[:, :, None] == jnp.arange(SPINS)[None, None, :]).astype(jnp.bfloat16)
    embed_term = jnp.einsum("mtv,mtd->vd", onehot, site_cot, preferred_element_type=jnp.float32)
    embed_term = jnp.where(section_index == 0, embed_term, jnp.zeros_like(embed_term))
    embed_grad = lax.psum(embed_term, ("samples", "section"))
    return (summed_weight[None], cotangents[None], embed_grad)


def solution(mesh):
    in_specs = (
        P("section", ("groups", "samples"), None, "mp"),
        P(("groups", "samples"), None, "mp"),
        P("section", "samples", "mp"),
        P("section", None, None),
        P(),
        P("groups"),
        P(("groups", "samples"), None),
    )
    out_specs = (
        P(("groups", "section"), "samples", "mp"),
        P("section", ("groups", "samples"), None, "mp"),
        P("groups", "mp"),
    )
    return jax.shard_map(local, mesh=mesh, in_specs=in_specs, out_specs=out_specs, check_vma=False)
```

profile of v0, /device:TPU:0, one launch (start us, length us, event | category | flops | bytes accessed | tf_op | source)
XLA Modules:
  0.0 230.9 jit_solution(3617918182335922141)
XLA Ops:
  7.2 0.7 all-gather.4.cloned.1.call-update
  8.0 1.1 fusion.20
  9.1 0.1 copy.44
  9.2 1.0 copy.68
  10.2 0.2 copy.48
  10.4 2.5 %all-gather = bf16[1,128,2048]{2,1,0:T(8,128)(2,1)S(1)} all-gather(bf16[1,128,1024]{2,1,0:T(8,128)(2,1)} %param.8), channel_id=2, replica_groups=mesh['groups'=2,'samples'=8,'section'=1,'mp'=2] {'mp'}, dimensions={2}, use_global_device_ids=true | all-gather | bytes 786432 | tf_op jit(solution)/shard_map/all_gather | solution.py:100
  13.0 0.4 fusion.78
  13.3 0.5 convolution_convert_fusion
  13.9 3.2 %convert_bitcast_fusion = bf16[2048,1024]{0,1:T(8,128)(2,1)} fusion(bf16[128,1024]{0,1:T(8,128)(2,1)S(1)} %bitcast.106, bf16[1,128,2048]{2,1,0:T(8,128)(2,1)S(1)} %all-gather), kind=kOutput, calls=%fused_computation.3 | convolution fusion | flops 538968064 | bytes 4980736 | tf_op jit(solution)/shard_map/mtf,mta->fa/dot_general | solution.py:119
  17.1 0.2 copy.49
  17.3 0.4 copy-done.1
  17.7 0.1 copy.58
  17.8 0.2 reduce-window.8
  18.0 0.6 dynamic_slice.12
  18.6 0.6 fusion.61
  19.3 66.3 %all-gather.4.cloned.1.call-done = bf16[1,2048,1024]{2,1,0:T(8,128)(2,1)} async-done(((bf16[1,256,1024]{2,1,0:T(8,128)(2,1)}), bf16[1,2048,1024]{2,1,0:T(8,128)(2,1)}) %all-gather.4.cloned.1.call-update) | async-done | bytes 4194320 | tf_op jit(solution)/shard_map/all_gather | solution.py:47
  85.6 2.9 %fusion.14 = bf16[16,8,8,128]{3,2,1,0:T(8,128)(2,1)S(1)} fusion(bf16[1,2048,1024]{2,1,0:T(8,128)(2,1)} %all-gather.4.cloned.1.call-done, bf16[1,128,2048]{2,1,0:T(8,128)(2,1)S(1)} %all-gather), kind=kOutput, calls=%fused_computation.19 | convolution fusion | flops 537001984 | bytes 4980736 | tf_op jit(solution)/shard_map/cond/branch_1_fun/dot_general | solution.py:68
  88.6 0.3 multiply_reduce_fusion
  89.0 0.3 fusion.81
  89.3 0.2 fusion.7
  89.5 0.5 fusion.5
  90.1 0.2 fusion.19
  90.3 1.2 fusion.23
  91.5 3.7 %all-to-all-start = ((bf16[8,1,64,1024]{3,2,1,0:T(8,128)(2,1)}), bf16[8,1,64,1024]{3,2,1,0:T(8,128)(2,1)S(1)}, u32[]{:S(2)}, u32[]{:S(2)}) async-start(bf16[8,1,64,1024]{3,2,1,0:T(8,128)(2,1)} %fusion.23), calls=%async_computation.1 | async-start | bytes 2097152 | tf_op jit(solution)/shard_map/all_to_all | solution.py:148
  95.3 103.4 %reduce-scatter.2.cloned.1.call-done = bf16[256,1024]{0,1:T(8,128)(2,1)} async-done(((bf16[2048,1024]{0,1:T(8,128)(2,1)}), bf16[256,1024]{0,1:T(8,128)(2,1)}) %reduce-scatter.2.cloned.1.call-update) | async-done | bytes 524304 | tf_op jit(solution)/shard_map/reduce_scatter | solution.py:118
  198.7 1.1 bitcast_convert_fusion
  199.8 1.3 copy.59
  201.1 0.8 fusion.24
  201.9 0.3 fusion.10
  202.2 0.2 fusion.35
  202.3 20.9 %psum.7 = f32[2,1024]{1,0:T(2,128)} all-reduce(f32[2,1024]{1,0:T(2,128)S(1)} %fusion.35), channel_id=1, replica_groups=mesh['groups'=2,'samples'=8,'section'=1,'mp'=2] {'samples','section'}, use_global_device_ids=true, to_apply=%region_5.6 | all-reduce | flops 2048 | bytes 16384 | tf_op jit(solution)/shard_map/psum | solution.py:160
  223.2 0.8 copy.60
  (17 shorter events, 0.4 us)
Async XLA Ops:
  7.2 78.5 %all-gather.4.cloned.1.call-start = ((), (), s32[]{:S(2)}) async-start(), calls=%async_computation.3 | async-start | bytes 4718592 | tf_op jit(solution)/shard_map/all_gather | solution.py:47
  7.9 190.8 %reduce-scatter.2.cloned.1.call-start = ((), (), s32[]{:S(2)}) async-start(), calls=%async_computation.2 | async-start | bytes 4718592 | tf_op jit(solution)/shard_map/reduce_scatter | solution.py:118
  13.9 3.2 %copy-start = (bf16[1,128,1024]{2,1,0:T(8,128)(2,1)S(1)}, bf16[1,128,1024]{2,1,0:T(8,128)(2,1)}, u32[]{:S(2)}) copy-start(bf16[1,128,1024]{2,1,0:T(8,128)(2,1)} %param.8) | copy-start | bytes 786436
  17.0 0.7 copy-start.1
  17.0 0.9 copy-start.3
  91.5 110.6 %copy-start.2 = (s32[1,128]{1,0:T(1,128)S(1)}, s32[1,128]{1,0:T(1,128)}, u32[]{:S(2)}) copy-start(s32[1,128]{1,0:T(1,128)} %param.13) | copy-start | bytes 1540
  91.5 109.6 %all-to-all-start = ((bf16[8,1,64,1024]{3,2,1,0:T(8,128)(2,1)}), bf16[8,1,64,1024]{3,2,1,0:T(8,128)(2,1)S(1)}, u32[]{:S(2)}, u32[]{:S(2)}) async-start(bf16[8,1,64,1024]{3,2,1,0:T(8,128)(2,1)} %fusion.23), calls=%async_computation.1 | async-start | bytes 2097152 | tf_op jit(solution)/shard_map/all_to_all | solution.py:148
Sparse Core Ops, SparseCore 0:
  10.1 75.4 all-gather.3
  89.3 109.3 reduce-scatter.1
where the time goes:
time: 231 us
  waiting for transfers between devices  170 us (74%)
  blocking collectives  23.4 us (10%)
  between operations  14.2 us (6%)
  matrix products  10.9 us (5%)
  local copies, waits for them, and re-layouts  4.81 us (2%)
  starting transfers between devices  3.76 us (2%)
  other arithmetic  3.48 us (2%)
    reduce_scatter x1, waiting for transfers between devices, local(): lax.psum_scatter(jnp.einsum('mtf,mta->fa', grad_store, attend_store, pref...  103 us
    all_gather x1, waiting for transfers between devices, local(): weights = lax.all_gather(layer_weights[0], 'samples', axis=0, tiled=True)  66.3 us
    psum x1, blocking collectives, local(): embed_grad = lax.psum(embed_term, ('samples', 'section'))  20.9 us
  transfers between devices with their start and end apart: 3, of which 2 were waited for; matrix products, arithmetic and copies ran while one was open for 7% of the time, Pallas kernels for 0%

commit v1 on v0

--- a/solution.py
+++ b/solution.py
@@ -157,7 +157,7 @@
     onehot = (spins[:, :, None] == jnp.arange(SPINS)[None, None, :]).astype(jnp.bfloat16)
     embed_term = jnp.einsum("mtv,mtd->vd", onehot, site_cot, preferred_element_type=jnp.float32)
     embed_term = jnp.where(section_index == 0, embed_term, jnp.zeros_like(embed_term))
-    embed_grad = lax.psum(embed_term, ("samples", "section"))
+    embed_grad = lax.psum(lax.psum(embed_term, "section"), "samples")
     return (summed_weight[None], cotangents[None], embed_grad)
 
 

time: 231 us -> 231 us (level)
  no operation moved by 1% of the time
where the time goes in v1:
time: 231 us
  waiting for transfers between devices  170 us (74%)
  blocking collectives  23.4 us (10%)
  between operations  14.2 us (6%)
  matrix products  10.9 us (5%)
  local copies, waits for them, and re-layouts  4.81 us (2%)
  starting transfers between devices  3.76 us (2%)
  other arithmetic  3.48 us (2%)
    reduce_scatter x1, waiting for transfers between devices, local(): lax.psum_scatter(jnp.einsum('mtf,mta->fa', grad_store, attend_store, pref...  103 us
    all_gather x1, waiting for transfers between devices, local(): weights = lax.all_gather(layer_weights[0], 'samples', axis=0, tiled=True)  66.3 us
    psum x1, blocking collectives, local(): embed_grad = lax.psum(lax.psum(embed_term, 'section'), 'samples')  20.9 us
  transfers between devices with their start and end apart: 3, of which 2 were waited for; matrix products, arithmetic and copies ran while one was open for 7% of the time, Pallas kernels for 0%

profile of v1, /device:TPU:0, one launch (start us, length us, event | category | flops | bytes accessed | tf_op | source)
XLA Modules:
  0.0 230.9 jit_solution(3617918182335922141)
XLA Ops:
  7.2 0.7 all-gather.4.cloned.1.call-update
  8.0 1.1 fusion.20
  9.1 0.1 copy.44
  9.2 1.0 copy.68
  10.2 0.2 copy.48
  10.4 2.5 %all-gather = bf16[1,128,2048]{2,1,0:T(8,128)(2,1)S(1)} all-gather(bf16[1,128,1024]{2,1,0:T(8,128)(2,1)} %param.8), channel_id=2, replica_groups=mesh['groups'=2,'samples'=8,'section'=1,'mp'=2] {'mp'}, dimensions={2}, use_global_device_ids=true | all-gather | bytes 786432 | tf_op jit(solution)/shard_map/all_gather | solution.py:100
  13.0 0.4 fusion.78
  13.3 0.5 convolution_convert_fusion
  13.9 3.2 %convert_bitcast_fusion = bf16[2048,1024]{0,1:T(8,128)(2,1)} fusion(bf16[128,1024]{0,1:T(8,128)(2,1)S(1)} %bitcast.106, bf16[1,128,2048]{2,1,0:T(8,128)(2,1)S(1)} %all-gather), kind=kOutput, calls=%fused_computation.3 | convolution fusion | flops 538968064 | bytes 4980736 | tf_op jit(solution)/shard_map/mtf,mta->fa/dot_general | solution.py:119
  17.1 0.2 copy.49
  17.3 0.4 copy-done.1
  17.7 0.1 copy.58
  17.8 0.2 reduce-window.8
  18.0 0.6 dynamic_slice.12
  18.6 0.6 fusion.61
  19.3 66.3 %all-gather.4.cloned.1.call-done = bf16[1,2048,1024]{2,1,0:T(8,128)(2,1)} async-done(((bf16[1,256,1024]{2,1,0:T(8,128)(2,1)}), bf16[1,2048,1024]{2,1,0:T(8,128)(2,1)}) %all-gather.4.cloned.1.call-update) | async-done | bytes 4194320 | tf_op jit(solution)/shard_map/all_gather | solution.py:47
  85.6 2.9 %fusion.14 = bf16[16,8,8,128]{3,2,1,0:T(8,128)(2,1)S(1)} fusion(bf16[1,2048,1024]{2,1,0:T(8,128)(2,1)} %all-gather.4.cloned.1.call-done, bf16[1,128,2048]{2,1,0:T(8,128)(2,1)S(1)} %all-gather), kind=kOutput, calls=%fused_computation.19 | convolution fusion | flops 537001984 | bytes 4980736 | tf_op jit(solution)/shard_map/cond/branch_1_fun/dot_general | solution.py:68
  88.6 0.3 multiply_reduce_fusion
  89.0 0.3 fusion.81
  89.3 0.2 fusion.7
  89.5 0.5 fusion.5
  90.1 0.2 fusion.19
  90.3 1.2 fusion.23
  91.5 3.7 %all-to-all-start = ((bf16[8,1,64,1024]{3,2,1,0:T(8,128)(2,1)}), bf16[8,1,64,1024]{3,2,1,0:T(8,128)(2,1)S(1)}, u32[]{:S(2)}, u32[]{:S(2)}) async-start(bf16[8,1,64,1024]{3,2,1,0:T(8,128)(2,1)} %fusion.23), calls=%async_computation.1 | async-start | bytes 2097152 | tf_op jit(solution)/shard_map/all_to_all | solution.py:148
  95.3 103.4 %reduce-scatter.2.cloned.1.call-done = bf16[256,1024]{0,1:T(8,128)(2,1)} async-done(((bf16[2048,1024]{0,1:T(8,128)(2,1)}), bf16[256,1024]{0,1:T(8,128)(2,1)}) %reduce-scatter.2.cloned.1.call-update) | async-done | bytes 524304 | tf_op jit(solution)/shard_map/reduce_scatter | solution.py:118
  198.7 1.1 bitcast_convert_fusion
  199.8 1.3 copy.59
  201.1 0.8 fusion.24
  201.9 0.3 fusion.10
  202.2 0.2 fusion.35
  202.3 20.9 %psum.6 = f32[2,1024]{1,0:T(2,128)} all-reduce(f32[2,1024]{1,0:T(2,128)S(1)} %fusion.35), channel_id=1, replica_groups=mesh['groups'=2,'samples'=8,'section'=1,'mp'=2] {'samples'}, use_global_device_ids=true, to_apply=%region_5.6 | all-reduce | flops 2048 | bytes 16384 | tf_op jit(solution)/shard_map/psum | solution.py:160
  223.2 0.8 copy.60
  (17 shorter events, 0.4 us)
Async XLA Ops:
  7.2 78.5 %all-gather.4.cloned.1.call-start = ((), (), s32[]{:S(2)}) async-start(), calls=%async_computation.3 | async-start | bytes 4718592 | tf_op jit(solution)/shard_map/all_gather | solution.py:47
  7.9 190.8 %reduce-scatter.2.cloned.1.call-start = ((), (), s32[]{:S(2)}) async-start(), calls=%async_computation.2 | async-start | bytes 4718592 | tf_op jit(solution)/shard_map/reduce_scatter | solution.py:118
  13.9 3.2 %copy-start = (bf16[1,128,1024]{2,1,0:T(8,128)(2,1)S(1)}, bf16[1,128,1024]{2,1,0:T(8,128)(2,1)}, u32[]{:S(2)}) copy-start(bf16[1,128,1024]{2,1,0:T(8,128)(2,1)} %param.8) | copy-start | bytes 786436
  17.0 0.7 copy-start.1
  17.0 0.9 copy-start.3
  91.5 110.6 %copy-start.2 = (s32[1,128]{1,0:T(1,128)S(1)}, s32[1,128]{1,0:T(1,128)}, u32[]{:S(2)}) copy-start(s32[1,128]{1,0:T(1,128)} %param.13) | copy-start | bytes 1540
  91.5 109.6 %all-to-all-start = ((bf16[8,1,64,1024]{3,2,1,0:T(8,128)(2,1)}), bf16[8,1,64,1024]{3,2,1,0:T(8,128)(2,1)S(1)}, u32[]{:S(2)}, u32[]{:S(2)}) async-start(bf16[8,1,64,1024]{3,2,1,0:T(8,128)(2,1)} %fusion.23), calls=%async_computation.1 | async-start | bytes 2097152 | tf_op jit(solution)/shard_map/all_to_all | solution.py:148
Sparse Core Ops, SparseCore 0:
  10.1 75.4 all-gather.3
  89.3 109.3 reduce-scatter.1
